TPU v7x, 32 devices: a whole 2x2x4 slice. The times are simulated.
32 devices in a mesh: view: 16 (over z, y, x), head: 2 (over core).
Axes of the slice: x: 2, y: 2, z: 4, core: 2. Of those that a mesh axis runs over, the one named last changes fastest.
Arguments:
- query_tokens: bfloat16 [4096, 1024], P('view'), may hold values from -360 to 360
- image_tokens: bfloat16 [16384, 1024], P('view'), may hold values from -6 to 6
- w_query: bfloat16 [1024, 1024], P(None, 'head'), may hold values from -0.1875 to 0.1875
- w_key: bfloat16 [1024, 1024], P(None, 'head'), may hold values from -0.1875 to 0.1875
- w_value: bfloat16 [1024, 1024], P(None, 'head'), may hold values from -0.1875 to 0.1875
- w_out: bfloat16 [1024, 1024], P('head'), may hold values from -0.1875 to 0.1875
- vis_list: int32 [32, 12], P('view'), may hold values from 0 to 127, as said below
- vis_count: int32 [32], P('view'), may hold values from 8 to 12
Outputs:
- attended: bfloat16 [4096, 1024], P('view', 'head')
Inputs may be any that keep to these rules, and one draw needn't show every extreme that they name: `vis_list`: entry j of row b names a global image block (block g holds image tokens g * 128 onward); the first vis_count[b] entries are the visible ones, the rest padding. All entries of one row lie on different devices of view. Among all entries of the 2 rows held by one device, those lying on one source device name the same block.
All inputs are finite; a program needn't handle non-finite values.
Results may differ from a plain program's by a relative error of at most 0.0085.
The roundings to bfloat16 on the way count: a program that leaves them out, or rounds other values in their place, can miss the bound.
Values may be sent and summed in bfloat16 or wider, within the bound.
A program may use at most 64 MiB of HBM per device.

v0:
```python
import math
import jax
import jax.numpy as jnp
from jax import lax
from jax.sharding import PartitionSpec as P

HEAD_DIM = 128
BLOCK = 128


def attend(query_heads, key_rows, visible, panel_width, head_count):
    groups, length = (key_rows.shape[0], key_rows.shape[1])
    key_heads = key_rows[:, :, :panel_width].reshape(groups, length, head_count, HEAD_DIM)
    value_heads = key_rows[:, :, panel_width:].reshape(groups, length, head_count, HEAD_DIM)
    scores = jnp.einsum(
        "qihd,qkhd->qhik", query_heads, key_heads, preferred_element_type=jnp.float32
    )
    scores = scores * (1.0 / math.sqrt(HEAD_DIM))
    allowed = visible[:, None, None, :]
    peak = jnp.max(jnp.where(allowed, scores, -1e30), axis=3, keepdims=True)
    raised = jnp.where(allowed, jnp.exp(scores - peak), 0.0)
    probs = (raised / jnp.sum(raised, axis=3, keepdims=True)).astype(jnp.bfloat16)
    context = jnp.einsum("qhik,qkhd->qihd", probs, value_heads, preferred_element_type=jnp.float32)
    return context.astype(jnp.bfloat16)


def per_device(query_tokens, image_tokens, w_query, w_key, w_value, w_out, vis_list, vis_count):
    view_count = lax.axis_size("view")
    panel_width = w_query.shape[1]
    head_count = panel_width // HEAD_DIM
    block_count = image_tokens.shape[0] // BLOCK
    query_blocks = vis_list.shape[0]
    queries = jnp.dot(query_tokens, w_query, preferred_element_type=jnp.float32).astype(
        jnp.bfloat16
    )
    image_keys = jnp.dot(image_tokens, w_key, preferred_element_type=jnp.float32).astype(
        jnp.bfloat16
    )
    image_values = jnp.dot(image_tokens, w_value, preferred_element_type=jnp.float32).astype(
        jnp.bfloat16
    )
    image_tiles = jnp.concatenate([image_keys, image_values], axis=1).reshape(
        block_count, BLOCK, 2 * panel_width
    )
    source = vis_list // block_count
    local_index = vis_list % block_count
    listed = jnp.arange(vis_list.shape[1], dtype=jnp.int32)[None, :] < vis_count[:, None]
    view_ids = jnp.arange(view_count, dtype=jnp.int32)
    matches = source[:, :, None] == view_ids[None, None, :]
    wanted = jnp.sum(jnp.where(matches, local_index[:, :, None], 0), axis=1)
    sourced = jnp.any(matches & listed[:, :, None], axis=1)
    asked_ids = lax.all_to_all(wanted, "view", split_axis=1, concat_axis=1, tiled=True)
    picked = jnp.take(image_tiles, asked_ids, axis=0)
    arrived = lax.all_to_all(picked, "view", split_axis=1, concat_axis=1, tiled=True)
    groups = arrived.shape[0]
    query_heads = queries.reshape(query_blocks, BLOCK, head_count, HEAD_DIM)
    key_rows = arrived.reshape(groups, -1, 2 * panel_width)
    visible = jnp.repeat(sourced, BLOCK, axis=1)
    context = attend(query_heads, key_rows, visible, panel_width, head_count)
    context = context.reshape(query_blocks * BLOCK, panel_width)
    partial_value = jnp.dot(context, w_out, preferred_element_type=jnp.float32)
    return lax.psum_scatter(partial_value, "head", scatter_dimension=1, tiled=True).astype(
        jnp.bfloat16
    )


def solution(mesh):
    return jax.shard_map(
        per_device,
        mesh=mesh,
        in_specs=(
            P("view", None),
            P("view", None),
            P(None, "head"),
            P(None, "head"),
            P(None, "head"),
            P("head", None),
            P("view", None),
            P("view"),
        ),
        out_specs=P("view", "head"),
        check_vma=False,
    )
```

profile of v0, /device:TPU:0, one launch (start us, length us, event | category | flops | bytes accessed | tf_op | source)
XLA Modules:
  0.0 303.1 jit_solution(4576486626460102009)
XLA Ops:
  6.5 0.0 copy-start
  6.5 0.0 copy-start.5
  6.5 0.8 and_select_fusion.1
  7.4 0.1 select_reduce_fusion.1
  7.5 0.7 copy.27
  8.2 8.3 %all-to-all-start = ((s32[2,16,1]{0,2,1:T(1,128)}), s32[2,16,1]{0,2,1:T(1,128)S(1)}, u32[]{:S(2)}, u32[]{:S(2)}) async-start(s32[2,16,1]{0,2,1:T(1,128)} %copy.27), calls=%async_computation | async-start | bytes 16384 | tf_op jit(solution)/shard_map/all_to_all | solution.py:52
  16.5 0.0 copy-done
  16.5 2.5 convolution_convert_fusion
  19.0 0.0 copy-done.5
  19.1 1.3 convolution_convert_fusion.1
  20.4 1.5 pad_maximum_fusion
  21.9 2.9 copy.38
  24.8 0.0 all-to-all-done
  24.8 0.1 copy.30
  24.9 0.1 reshape.58
  25.0 0.1 copy.28
  25.1 0.1 copy.29
  25.2 4.8 %gather_fusion = bf16[32,128,1024]{2,1,0:T(8,128)(2,1)} fusion(bf16[8,128,1024]{2,1,0:T(8,128)(2,1)S(1)} %bitcast.34, s32[1024]{0:T(1024)S(1)} %pad_clamp_fusion), kind=kCustom, calls=%fused_computation | custom fusion | bytes 16777344 | tf_op jit(solution)/shard_map/jit(_take)/gather | solution.py:53
  30.0 7.5 %copy_select_fusion = bf16[2,16,128,1024]{3,2,0,1:T(8,128)(2,1)} fusion(bf16[2,16,128,1024]{3,2,1,0:T(8,128)(2,1)} %bitcast.35, pred[2,16]{0,1:T(8,128)(4,1)S(1)} %copy.29), kind=kLoop, calls=%fused_computation.2 | loop fusion | flops 4194304 | bytes 16777248 | tf_op jit(solution)/shard_map/jit(_take)/select_n | solution.py:53
  37.5 0.0 copy-start.6
  37.5 0.0 copy-start.2
  37.5 0.0 copy-start.4
  37.5 7.1 %all-to-all-start.1 = ((bf16[2,16,128,1024]{3,2,0,1:T(8,128)(2,1)}), bf16[2,16,128,1024]{3,2,0,1:T(8,128)(2,1)}, u32[]{:S(2)}, u32[]{:S(2)}) async-start(bf16[2,16,128,1024]{3,2,0,1:T(8,128)(2,1)} %copy_select_fusion), calls=%async_computation.1 | async-start | bytes 16777216 | tf_op jit(solution)/shard_map/all_to_all | solution.py:54
  44.6 0.2 reduce-scatter.2.cloned.1.call-start
  44.8 0.0 copy-done.6
  44.8 0.1 iota_compare_fusion.1
  44.9 0.1 fusion.24
  45.0 0.1 broadcast_bitcast_fusion
  45.1 0.0 copy-done.2
  45.1 0.0 copy-done.4
  45.1 0.4 convolution_convert_fusion.2
  45.5 0.1 reshape.53
  45.6 154.6 %all-to-all-done.1 = bf16[2,16,128,1024]{3,2,0,1:T(8,128)(2,1)} async-done(((bf16[2,16,128,1024]{3,2,0,1:T(8,128)(2,1)}), bf16[2,16,128,1024]{3,2,0,1:T(8,128)(2,1)}, u32[]{:S(2)}, u32[]{:S(2)}) %all-to-all-start.1) | async-done | bytes 8388640 | tf_op jit(solution)/shard_map/all_to_all | solution.py:54
  200.2 12.6 %copy.33 = bf16[2,16,128,1024]{2,1,3,0:T(8,128)(2,1)} copy(bf16[2,16,128,1024]{3,2,0,1:T(8,128)(2,1)} %all-to-all-done.1) | data formatting | bytes 16777216 | tf_op jit(solution)/shard_map/all_to_all | solution.py:54
  212.8 13.3 %reshape.51 = bf16[2,2048,1024]{1,2,0:T(8,128)(2,1)} reshape(bf16[2,16,128,1024]{2,1,3,0:T(8,128)(2,1)} %copy.33) | data formatting | bytes 16777216 | tf_op jit(solution)/shard_map/reshape | solution.py:57
  226.1 6.0 %fusion.27 = (bf16[2,2048,512]{1,2,0:T(8,128)(2,1)}, bf16[2,2048,512]{1,2,0:T(8,128)(2,1)}) fusion(bf16[2,2048,1024]{1,2,0:T(8,128)(2,1)} %reshape.51), kind=kLoop, calls=%fused_computation.44 | loop fusion | bytes 16777216 | tf_op jit(solution)/shard_map/slice | solution.py:13
  232.1 10.6 %fusion.28 = (f32[2,4,128]{2,1,0:T(4,128)S(1)}, f32[2,4,128,2048]{3,2,1,0:T(8,128)}) fusion(pred[2,2048]{1,0:T(4,128)(4,1)S(1)} %bitcast.39, bf16[2,2048,4,128]{1,3,2,0:T(8,128)(2,1)} %bitcast.37, bf16[2,128,4,128]{3,2,1,0:T(4,128)(2,1)S(1)} %reshape.53), kind=kOutput, calls=%fused_computation.45 | convolution fusion | flops 1086326784 | bytes 12853248 | tf_op jit(solution)/shard_map/sub | solution.py:21
  242.7 0.0 copy-start.3
  242.7 0.0 copy-start.1
  242.7 6.8 %fusion.10 = bf16[2,128,4,128]{1,3,2,0:T(8,128)(2,1)} fusion(bf16[2,2048,4,128]{1,3,2,0:T(8,128)(2,1)} %bitcast.36, f32[2,4,128,2048]{3,2,1,0:T(8,128)} %get-tuple-element.12, f32[2,4,128]{2,1,0:T(4,128)S(1)} %get-tuple-element.11), kind=kOutput, calls=%fused_computation.17 | convolution fusion | flops 541196288 | bytes 12849152 | tf_op jit(solution)/shard_map/qhik,qkhd->qihd/dot_general | solution.py:23
  249.5 1.1 copy.36
  250.6 0.0 copy-done.3
  250.7 1.4 fusion.13
  252.1 0.0 reduce-scatter.2.cloned.1.call-update
  252.1 42.3 %reduce-scatter.2.cloned.1.call-done = f32[256,512]{1,0:T(8,128)} async-done(((f32[256,1024]{1,0:T(8,128)}), f32[256,512]{1,0:T(8,128)}) %reduce-scatter.2.cloned.1.call-update) | async-done | bytes 524304 | tf_op jit(solution)/shard_map/reduce_scatter | solution.py:62
  294.4 1.8 convert_element_type.27
  296.2 0.0 copy-done.1
  (3 shorter events, 0.0 us)
Async XLA Ops:
  6.5 10.0 %copy-start = (bf16[1024,1024]{1,0:T(8,128)(2,1)S(1)}, bf16[1024,1024]{1,0:T(8,128)(2,1)}, u32[]{:S(2)}) copy-start(bf16[1024,1024]{1,0:T(8,128)(2,1)} %param.9) | copy-start | bytes 6291460
  6.5 12.5 %copy-start.5 = (bf16[1024,512]{1,0:T(8,128)(2,1)S(1)}, bf16[1024,512]{1,0:T(8,128)(2,1)}, u32[]{:S(2)}) copy-start(bf16[1024,512]{1,0:T(8,128)(2,1)} %param.11) | copy-start | bytes 3145732
  8.2 16.6 %all-to-all-start = ((s32[2,16,1]{0,2,1:T(1,128)}), s32[2,16,1]{0,2,1:T(1,128)S(1)}, u32[]{:S(2)}, u32[]{:S(2)}) async-start(s32[2,16,1]{0,2,1:T(1,128)} %copy.27), calls=%async_computation | async-start | bytes 16384 | tf_op jit(solution)/shard_map/all_to_all | solution.py:52
  37.5 7.3 %copy-start.6 = (s32[2]{0:T(128)S(1)}, s32[2]{0:T(128)}, u32[]{:S(2)}) copy-start(s32[2]{0:T(128)} %param.15) | copy-start | bytes 28
  37.5 7.6 %copy-start.2 = (bf16[1024,512]{1,0:T(8,128)(2,1)S(1)}, bf16[1024,512]{1,0:T(8,128)(2,1)}, u32[]{:S(2)}) copy-start(bf16[1024,512]{1,0:T(8,128)(2,1)} %param.10) | copy-start | bytes 3145732
  37.5 7.6 %copy-start.4 = (bf16[256,1024]{1,0:T(8,128)(2,1)S(1)}, bf16[256,1024]{1,0:T(8,128)(2,1)}, u32[]{:S(2)}) copy-start(bf16[256,1024]{1,0:T(8,128)(2,1)} %param.8) | copy-start | bytes 1572868
  37.5 162.7 %all-to-all-start.1 = ((bf16[2,16,128,1024]{3,2,0,1:T(8,128)(2,1)}), bf16[2,16,128,1024]{3,2,0,1:T(8,128)(2,1)}, u32[]{:S(2)}, u32[]{:S(2)}) async-start(bf16[2,16,128,1024]{3,2,0,1:T(8,128)(2,1)} %copy_select_fusion), calls=%async_computation.1 | async-start | bytes 16777216 | tf_op jit(solution)/shard_map/all_to_all | solution.py:54
  44.6 249.9 %reduce-scatter.2.cloned.1.call-start = ((), (), s32[]{:S(2)}) async-start(), calls=%async_computation.3 | async-start | bytes 1572864 | tf_op jit(solution)/shard_map/reduce_scatter | solution.py:62
  242.7 8.0 %copy-start.3 = (bf16[512,1024]{1,0:T(8,128)(2,1)S(1)}, bf16[512,1024]{1,0:T(8,128)(2,1)}, u32[]{:S(2)}) copy-start(bf16[512,1024]{1,0:T(8,128)(2,1)} %param.13) | copy-start | bytes 3145732
  242.7 53.6 %copy-start.1 = (bf16[1024,1024]{1,0:T(8,128)(2,1)S(1)}, bf16[1024,1024]{1,0:T(8,128)(2,1)}, u32[]{:S(2)}) copy-start(bf16[1024,1024]{1,0:T(8,128)(2,1)} %param.9) | copy-start | bytes 6291460
Sparse Core Ops, SparseCore 0:
  252.2 42.1 reduce-scatter.1
where the time goes:
time: 304 us; the launch traced here: 303 us
  waiting for transfers between devices  197 us (65%)
  local copies, waits for them, and re-layouts  41.9 us (14%)
  matrix products  23.1 us (8%)
  starting transfers between devices  15.6 us (5%)
  between operations  13.5 us (4%)
  other arithmetic  11.9 us (4%)
    all_to_all x1, waiting for transfers between devices, per_device(): lax.all_to_all(picked, 'view', split_axis=1, concat_axis=1, tiled=True)  155 us
    reduce_scatter x1, waiting for transfers between devices, per_device(): lax.psum_scatter(partial_value, 'head', scatter_dimension=1, tiled=True)  42.3 us
    reshape x1, local copies, waits for them, and re-layouts, per_device(): key_rows = arrived.reshape(groups, -1, 2 * panel_width)  13.3 us
    all_to_all x1, local copies, waits for them, and re-layouts, per_device(): lax.all_to_all(picked, 'view', split_axis=1, concat_axis=1, tiled=True)  12.6 us
    sub x1, matrix products, attend(): raised = jnp.where(allowed, jnp.exp(scores - peak), 0.0)  10.6 us
    all_to_all x1, starting transfers between devices, per_device(): lax.all_to_all(wanted, 'view', split_axis=1, concat_axis=1, tiled=True)  8.34 us
    select_n x1, other arithmetic, per_device(): picked = jnp.take(image_tiles, asked_ids, axis=0)  7.47 us
    all_to_all x1, starting transfers between devices, per_device(): lax.all_to_all(picked, 'view', split_axis=1, concat_axis=1, tiled=True)  7.08 us
  transfers between devices with their start and end apart: 3, of which 2 were waited for; matrix products, arithmetic and copies ran while one was open for 3% of the time, Pallas kernels for 0%

commit v1 on v0

--- a/solution.py
+++ b/solution.py
@@ -51,7 +51,10 @@
     sourced = jnp.any(matches & listed[:, :, None], axis=1)
     asked_ids = lax.all_to_all(wanted, "view", split_axis=1, concat_axis=1, tiled=True)
     picked = jnp.take(image_tiles, asked_ids, axis=0)
-    arrived = lax.all_to_all(picked, "view", split_axis=1, concat_axis=1, tiled=True)
+    arrived = jnp.concatenate(
+        lax.all_to_all(jnp.stack(jnp.split(picked, lax.axis_size("view"), axis=1)), "view", 0, 0),
+        axis=1,
+    )
     groups = arrived.shape[0]
     query_heads = queries.reshape(query_blocks, BLOCK, head_count, HEAD_DIM)
     key_rows = arrived.reshape(groups, -1, 2 * panel_width)

time: 304 us -> 330 us (1.086)
  local copies, waits for them, and re-layouts: 41.9 us -> 66.6 us
    unnamed x16 -> x29, local copies, waits for them, and re-layouts: 0.12 us -> 28.2 us
    all_to_all x1 -> x0, local copies, waits for them, and re-layouts: 12.6 us -> none  [per_device(): lax.all_to_all(picked, 'view', split_axis=1, concat_axis=1, tiled=True)]
    slice x0 -> x1, local copies, waits for them, and re-layouts: none -> 6.31 us  [attend(): key_rows[:, :, panel_width:].reshape(groups, length, head_count, HEAD_DIM)]
    slice x1 -> x2, local copies, waits for them, and re-layouts: 6 us -> 12 us  [attend(): key_rows[:, :, :panel_width].reshape(groups, length, head_count, HEAD_DIM)]
    reshape x1, local copies, waits for them, and re-layouts: 13.3 us -> 8.25 us  [per_device(): jnp.concatenate(lax.all_to_all(jnp.stack(jnp.split(picked, lax.axis_size(...]
where the time goes in v1:
time: 330 us; the launch traced here: 329 us
  waiting for transfers between devices  197 us (60%)
  local copies, waits for them, and re-layouts  66.6 us (20%)
  matrix products  24.2 us (7%)
  starting transfers between devices  15.7 us (5%)
  between operations  13.5 us (4%)
  other arithmetic  11.9 us (4%)
    all_to_all x1, waiting for transfers between devices, per_device(): lax.all_to_all(jnp.stack(jnp.split(picked, lax.axis_size('view'), axis=1)...  155 us
    reduce_scatter x1, waiting for transfers between devices, per_device(): lax.psum_scatter(partial_value, 'head', scatter_dimension=1, tiled=True)  42.4 us
    unnamed x29, local copies, waits for them, and re-layouts  28.2 us
    slice x2, local copies, waits for them, and re-layouts, attend(): key_rows[:, :, :panel_width].reshape(groups, length, head_count, HEAD_DIM)  12 us
    sub x1, matrix products, attend(): raised = jnp.where(allowed, jnp.exp(scores - peak), 0.0)  10.5 us
    all_to_all x1, starting transfers between devices, per_device(): lax.all_to_all(wanted, 'view', split_axis=1, concat_axis=1, tiled=True)  8.34 us
    reshape x1, local copies, waits for them, and re-layouts, per_device(): jnp.concatenate(lax.all_to_all(jnp.stack(jnp.split(picked, lax.axis_size(...  8.25 us
    select_n x1, other arithmetic, per_device(): picked = jnp.take(image_tiles, asked_ids, axis=0)  7.47 us
  transfers between devices with their start and end apart: 3, of which 2 were waited for; matrix products, arithmetic and copies ran while one was open for 3% of the time, Pallas kernels for 0%

profile of v1, /device:TPU:0, one launch (start us, length us, event | category | flops | bytes accessed | tf_op | source)
XLA Modules:
  0.0 328.9 jit_solution(3050426945798820937)
XLA Ops:
  6.5 0.8 and_select_fusion.1
  7.4 0.1 select_reduce_fusion.1
  7.5 0.7 copy.54
  8.2 8.3 %all-to-all-start = ((s32[2,16,1]{0,2,1:T(1,128)}), s32[2,16,1]{0,2,1:T(1,128)S(1)}, u32[]{:S(2)}, u32[]{:S(2)}) async-start(s32[2,16,1]{0,2,1:T(1,128)} %copy.54), calls=%async_computation | async-start | bytes 16384 | tf_op jit(solution)/shard_map/all_to_all | solution.py:52
  16.5 2.5 convolution_convert_fusion
  19.0 2.5 convolution_convert_fusion.1
  21.6 1.5 pad_maximum_fusion
  23.1 2.9 copy.67
  26.0 0.1 copy.57
  26.0 0.1 reshape.58
  26.1 0.1 copy.55
  26.2 0.1 copy.56
  26.3 4.8 %gather_fusion = bf16[32,128,1024]{2,1,0:T(8,128)(2,1)} fusion(bf16[8,128,1024]{2,1,0:T(8,128)(2,1)S(1)} %bitcast.96, s32[1024]{0:T(1024)S(1)} %pad_clamp_fusion), kind=kCustom, calls=%fused_computation | custom fusion | bytes 16777344 | tf_op jit(solution)/shard_map/jit(_take)/gather | solution.py:53
  31.2 7.5 %copy_select_fusion = bf16[2,16,128,1024]{3,2,0,1:T(8,128)(2,1)} fusion(bf16[2,16,128,1024]{3,2,1,0:T(8,128)(2,1)} %bitcast.97, pred[2,16]{0,1:T(8,128)(4,1)S(1)} %copy.56), kind=kLoop, calls=%fused_computation.2 | loop fusion | flops 4194304 | bytes 16777248 | tf_op jit(solution)/shard_map/jit(_take)/select_n | solution.py:53
  38.6 1.9 fusion.28
  40.5 1.9 fusion.27
  42.4 1.9 fusion.26
  44.3 1.9 fusion.25
  46.1 1.9 fusion.24
  48.0 1.9 fusion.23
  49.9 1.9 fusion.22
  51.7 1.9 fusion.21
  53.6 1.9 fusion.20
  55.5 1.9 fusion.19
  57.4 1.9 fusion.18
  59.3 1.9 fusion.17
  61.1 1.9 fusion.16
  63.0 1.9 fusion.15
  64.9 1.9 fusion.14
  66.8 1.9 fusion.13
  68.7 7.1 %all-to-all-start.1 = ((bf16[16,2,1,128,1024]{4,3,1,2,0:T(8,128)(2,1)}), bf16[16,2,1,128,1024]{4,3,1,2,0:T(8,128)(2,1)}, u32[]{:S(2)}, u32[]{:S(2)}) async-start(bf16[16,2,1,128,1024]{4,3,1,2,0:T(8,128)(2,1)} %fusion.13), calls=%async_computation.1 | async-start | bytes 16777216 | tf_op jit(solution)/shard_map/all_to_all | solution.py:55
  75.8 0.2 reduce-scatter.2.cloned.1.call-start
  76.0 0.1 iota_compare_fusion.1
  76.1 0.1 fusion.40
  76.2 0.1 broadcast_bitcast_fusion
  76.3 0.4 convolution_convert_fusion.2
  76.7 0.1 reshape.53
  76.8 154.5 %all-to-all-done.1 = bf16[16,2,1,128,1024]{4,3,1,2,0:T(8,128)(2,1)} async-done(((bf16[16,2,1,128,1024]{4,3,1,2,0:T(8,128)(2,1)}), bf16[16,2,1,128,1024]{4,3,1,2,0:T(8,128)(2,1)}, u32[]{:S(2)}, u32[]{:S(2)}) %all-to-all-start.1) | async-done | bytes 8388640 | tf_op jit(solution)/shard_map/all_to_all | solution.py:55
  231.3 8.3 %copy.60 = bf16[2,16,1,128,1024]{4,3,1,0,2:T(8,128)(2,1)} copy(bf16[2,16,1,128,1024]{4,3,0,2,1:T(8,128)(2,1)} %bitcast.20) | data formatting | bytes 16777216 | tf_op jit(solution)/shard_map/reshape | solution.py:54
  239.6 5.8 %fusion.43 = (bf16[2,2048,512]{2,1,0:T(8,128)(2,1)}, bf16[2,2048,512]{2,1,0:T(8,128)(2,1)}) fusion(bf16[2,2048,1024]{2,1,0:T(8,128)(2,1)} %bitcast.98), kind=kLoop, calls=%fused_computation.76 | loop fusion | bytes 16777216 | tf_op jit(solution)/shard_map/slice | solution.py:13
  245.3 6.2 %copy.62 = bf16[2,2048,512]{1,2,0:T(8,128)(2,1)} copy(bf16[2,2048,512]{2,1,0:T(8,128)(2,1)} %get-tuple-element.7) | data formatting | bytes 8388608 | tf_op jit(solution)/shard_map/slice | solution.py:13
  251.6 6.3 %copy.61 = bf16[2,2048,512]{1,2,0:T(8,128)(2,1)} copy(bf16[2,2048,512]{2,1,0:T(8,128)(2,1)} %get-tuple-element.8) | data formatting | bytes 8388608 | tf_op jit(solution)/shard_map/slice | solution.py:14
  257.9 10.5 %fusion.44 = (f32[2,4,128]{2,1,0:T(4,128)S(1)}, f32[2,4,128,2048]{3,2,1,0:T(8,128)}) fusion(pred[2,2048]{1,0:T(4,128)(4,1)S(1)} %bitcast.102, bf16[2,2048,4,128]{1,3,2,0:T(8,128)(2,1)} %bitcast.99, bf16[2,128,4,128]{3,2,1,0:T(4,128)(2,1)S(1)} %reshape.53), kind=kOutput, calls=%fused_computation.77 | convolution fusion | flops 1086326784 | bytes 12853248 | tf_op jit(solution)/shard_map/sub | solution.py:21
  268.4 6.8 %fusion.10 = bf16[2,128,4,128]{1,3,2,0:T(8,128)(2,1)} fusion(bf16[2,2048,4,128]{1,3,2,0:T(8,128)(2,1)} %bitcast.100, f32[2,4,128,2048]{3,2,1,0:T(8,128)} %get-tuple-element.12, f32[2,4,128]{2,1,0:T(4,128)S(1)} %get-tuple-element.11), kind=kOutput, calls=%fused_computation.17 | convolution fusion | flops 541196288 | bytes 12849152 | tf_op jit(solution)/shard_map/qhik,qkhd->qihd/dot_general | solution.py:23
  275.3 1.1 copy.65
  276.4 1.4 fusion.29
  277.9 42.4 %reduce-scatter.2.cloned.1.call-done = f32[256,512]{1,0:T(8,128)} async-done(((f32[256,1024]{1,0:T(8,128)}), f32[256,512]{1,0:T(8,128)}) %reduce-scatter.2.cloned.1.call-update) | async-done | bytes 524304 | tf_op jit(solution)/shard_map/reduce_scatter | solution.py:65
  320.2 1.8 convert_element_type.27
  (17 shorter events, 0.1 us)
Async XLA Ops:
  6.5 10.0 %copy-start = (bf16[1024,1024]{1,0:T(8,128)(2,1)S(1)}, bf16[1024,1024]{1,0:T(8,128)(2,1)}, u32[]{:S(2)}) copy-start(bf16[1024,1024]{1,0:T(8,128)(2,1)} %param.9) | copy-start | bytes 6291460
  8.2 17.8 %all-to-all-start = ((s32[2,16,1]{0,2,1:T(1,128)}), s32[2,16,1]{0,2,1:T(1,128)S(1)}, u32[]{:S(2)}, u32[]{:S(2)}) async-start(s32[2,16,1]{0,2,1:T(1,128)} %copy.54), calls=%async_computation | async-start | bytes 16384 | tf_op jit(solution)/shard_map/all_to_all | solution.py:52
  68.7 7.3 %copy-start.5 = (s32[2]{0:T(128)S(1)}, s32[2]{0:T(128)}, u32[]{:S(2)}) copy-start(s32[2]{0:T(128)} %param.15) | copy-start | bytes 28
  68.7 7.6 %copy-start.2 = (bf16[1024,512]{1,0:T(8,128)(2,1)S(1)}, bf16[1024,512]{1,0:T(8,128)(2,1)}, u32[]{:S(2)}) copy-start(bf16[1024,512]{1,0:T(8,128)(2,1)} %param.10) | copy-start | bytes 3145732
  68.7 7.6 %copy-start.4 = (bf16[256,1024]{1,0:T(8,128)(2,1)S(1)}, bf16[256,1024]{1,0:T(8,128)(2,1)}, u32[]{:S(2)}) copy-start(bf16[256,1024]{1,0:T(8,128)(2,1)} %param.8) | copy-start | bytes 1572868
  68.7 162.7 %all-to-all-start.1 = ((bf16[16,2,1,128,1024]{4,3,1,2,0:T(8,128)(2,1)}), bf16[16,2,1,128,1024]{4,3,1,2,0:T(8,128)(2,1)}, u32[]{:S(2)}, u32[]{:S(2)}) async-start(bf16[16,2,1,128,1024]{4,3,1,2,0:T(8,128)(2,1)} %fusion.13), calls=%async_computation.1 | async-start | bytes 16777216 | tf_op jit(solution)/shard_map/all_to_all | solution.py:55
  75.8 244.5 %reduce-scatter.2.cloned.1.call-start = ((), (), s32[]{:S(2)}) async-start(), calls=%async_computation.3 | async-start | bytes 1572864 | tf_op jit(solution)/shard_map/reduce_scatter | solution.py:65
  268.4 8.0 %copy-start.3 = (bf16[512,1024]{1,0:T(8,128)(2,1)S(1)}, bf16[512,1024]{1,0:T(8,128)(2,1)}, u32[]{:S(2)}) copy-start(bf16[512,1024]{1,0:T(8,128)(2,1)} %param.13) | copy-start | bytes 3145732
  268.4 53.6 %copy-start.1 = (bf16[1024,1024]{1,0:T(8,128)(2,1)S(1)}, bf16[1024,1024]{1,0:T(8,128)(2,1)}, u32[]{:S(2)}) copy-start(bf16[1024,1024]{1,0:T(8,128)(2,1)} %param.9) | copy-start | bytes 6291460
Sparse Core Ops, SparseCore 0:
  278.0 42.2 reduce-scatter.1
